TPU v7x, 32 devices: a whole 2x2x4 slice. The times are simulated.
32 devices in a mesh: tile: 8 (over y, x, core), member: 4 (over z).
Axes of the slice: x: 2, y: 2, z: 4, core: 2. Of those that a mesh axis runs over, the one named last changes fastest.
Arguments:
- hx: bfloat16 [512, 32768], P('member', 'tile'), may hold values from -6 to 6
- obs_value: bfloat16 [32768], P('tile'), may hold values from -8 to 8
- obs_rinv: bfloat16 [32768], P('tile'), may hold values from 0.29882812 to 4
- obs_index: int32 [32, 1024], P('tile'), may hold values from 512 to 5631, as said below
- loc_weight: float32 [32, 1024], P(('tile', 'member')), may hold values from 0.05 to 1
- state: bfloat16 [512, 131072], P('member', 'tile'), may hold values from -6 to 6
Outputs:
- analysis: bfloat16 [512, 131072], P('member', 'tile')
Inputs may be any that keep to these rules, and one draw needn't show every extreme that they name: `obs_index`: row p lists 1024 distinct positions in the pool of tile p // 4: positions 0 .. 1023 are the last 1024 observations of the tile before it, the next 4096 the tile's own, the last 1024 the first observations of the tile after it; the tiles form a closed band. All positions of a row lie within 2048 consecutive positions.
All inputs are finite; a program needn't handle non-finite values.
Results may differ from a plain program's by a relative error of at most 0.012.
The roundings to bfloat16 on the way count: a program that leaves them out, or rounds other values in their place, can miss the bound.
Values may be sent and summed in bfloat16 or wider, within the bound.
No kernel may reach another device: no remote copies, remote signals or barrier semaphores. Data moves between devices by JAX's collectives and lax.ppermute only.
A program may use at most 64 MiB of HBM per device.

v0:
```python
import jax
import jax.numpy as jnp
from jax import lax
from jax.sharding import PartitionSpec as P

LOC = 1024
NS_ITERS = 3


def with_halo(block, sides, width):
    for axis, dim in sides:
        count = lax.axis_size(axis)
        forward = [(i, i + 1) for i in range(count - 1)]
        forward.append((count - 1, 0))
        backward = [(target, source) for source, target in forward]
        low = lax.ppermute(
            lax.slice_in_dim(block, block.shape[dim] - width, None, axis=dim), axis, forward
        )
        high = lax.ppermute(lax.slice_in_dim(block, 0, width, axis=dim), axis, backward)
        block = jnp.concatenate([low, block, high], axis=dim)
    return block


def product_f32(left, right, dims):
    return lax.dot_general(
        left.astype(jnp.float32),
        right.astype(jnp.float32),
        (dims, ((), ())),
        precision=lax.Precision.HIGHEST,
        preferred_element_type=jnp.float32,
    )


def analysis(obs_block, obs_pair, loc_row):
    members = obs_block.shape[0]
    block_f = obs_block.astype(jnp.float32)
    obs_mean = jnp.mean(block_f, axis=0)
    obs_root = jnp.sqrt(obs_pair[1].astype(jnp.float32) * loc_row)
    scaled = ((block_f - obs_mean) * obs_root).astype(jnp.bfloat16)
    innovation = (obs_pair[0].astype(jnp.float32) - obs_mean) * obs_root
    gram_matrix = product_f32(scaled, scaled, ((1,), (1,)))
    identity = jnp.eye(members, dtype=jnp.float32)
    system = gram_matrix + (members - 1.0) * identity
    projection = jnp.dot(scaled.astype(jnp.float32), innovation, precision=lax.Precision.HIGHEST)
    norm_a = jnp.sqrt(jnp.sum(system * system))
    upper_iter = system / norm_a
    lower_iter = identity
    for sweep in range(NS_ITERS):
        upper_b = upper_iter.astype(jnp.bfloat16)
        lower_b = lower_iter.astype(jnp.bfloat16)
        product = product_f32(lower_b, upper_b, ((1,), (0,)))
        half_step = (1.5 * identity - 0.5 * product).astype(jnp.bfloat16)
        if sweep + 1 < NS_ITERS:
            upper_iter = product_f32(upper_b, half_step, ((1,), (0,)))
        lower_iter = product_f32(half_step, lower_b, ((1,), (0,)))
    invroot = lower_iter / jnp.sqrt(norm_a)
    inner_w = jnp.dot(invroot, projection, precision=lax.Precision.HIGHEST)
    mean_w = jnp.dot(invroot, inner_w, precision=lax.Precision.HIGHEST)
    transform = jnp.sqrt(members - 1.0) * invroot + mean_w[:, None]
    return transform.astype(jnp.bfloat16)


def transform_state(transform, state_block):
    block_f = state_block.astype(jnp.float32)
    state_mean = jnp.mean(block_f, axis=0)
    state_pert = (block_f - state_mean).astype(jnp.bfloat16)
    combined = product_f32(transform, state_pert, ((0,), (0,)))
    return (state_mean + combined).astype(jnp.bfloat16)


def on_device(hx, obs_value, obs_rinv, obs_index, loc_weight, state):
    ens_dev = hx.shape[0]
    member_pos = lax.axis_index("member")
    stacked = jnp.concatenate([hx, obs_value[None, :], obs_rinv[None, :]], axis=0)
    obs_pool = with_halo(stacked, (("tile", 1),), LOC)
    own_index = lax.dynamic_index_in_dim(obs_index, member_pos, 0, keepdims=False)
    obs_pair = jnp.take(obs_pool[ens_dev:], own_index, axis=1)
    picked = jnp.take(obs_pool[:ens_dev], obs_index, axis=1)
    received = lax.all_to_all(picked, "member", split_axis=1, concat_axis=0, tiled=True)
    obs_block = received[:, 0, :]
    transform = analysis(obs_block, obs_pair, loc_weight[0])
    group_count = obs_index.shape[0]
    state_split = state.reshape(ens_dev, group_count, state.shape[1] // group_count)
    updated = transform_state(
        transform,
        lax.all_to_all(state_split, "member", split_axis=1, concat_axis=0, tiled=True)[:, 0, :],
    )
    result = lax.all_to_all(updated[:, None, :], "member", split_axis=0, concat_axis=1, tiled=True)
    return result.reshape(ens_dev, state.shape[1])


def solution(mesh):
    in_specs = (
        P("member", "tile"),
        P("tile"),
        P("tile"),
        P("tile", None),
        P(("tile", "member"), None),
        P("member", "tile"),
    )
    out_specs = P("member", "tile")
    return jax.shard_map(
        on_device, mesh=mesh, in_specs=in_specs, out_specs=out_specs, check_vma=False
    )
```

profile of v0, /device:TPU:0, one launch (start us, length us, event | category | flops | bytes accessed | tf_op | source)
XLA Modules:
  0.0 328.8 jit_solution(2803960686868438312)
XLA Ops:
  0.0 0.0 copy-start.1
  0.0 1.6 copy.52
  1.6 1.3 broadcast_in_dim.44
  2.9 1.3 broadcast_in_dim.45
  4.2 0.3 pad_maximum_fusion.3
  4.6 0.5 collective-permute-start
  5.1 2.9 collective-permute-start.1
  8.1 0.0 copy-done.1
  8.1 9.8 %collective-permute-done = bf16[130,1024]{0,1:T(8,128)(2,1)S(1)} collective-permute-done((bf16[130,1024]{0,1:T(8,128)(2,1)S(1)}, bf16[130,1024]{0,1:T(8,128)(2,1)S(1)}, u32[]{:S(2)}, u32[]{:S(2)}) %collective-permute-start) | collective-permute-done | bytes 266272 | tf_op jit(solution)/shard_map/ppermute | solution.py:16
  17.9 1.5 collective-permute-done.1
  19.3 10.2 %pad_maximum_fusion = bf16[130,6144]{0,1:T(8,128)(2,1)S(1)} fusion(bf16[130,1024]{0,1:T(8,128)(2,1)S(1)} %collective-permute-done.1, bf16[1,4096]{0,1:T(8,128)(2,1)S(1)} %broadcast_in_dim.45, bf16[1,4096]{0,1:T(8,128)(2,1)S(1)} %broadcast_in_dim.44, bf16[128,4096]{0,1:T(8,128)(2,1)S(1)} %copy.52, bf16[130,1024]{0,1:T(8,128)(2,1)S(1)} %collective-permute-done), kind=kLoop, calls=%fused_computation.7 | loop fusion | flops 7987200 | bytes 3194880 | tf_op jit(solution)/shard_map/concatenate | solution.py:20
  29.5 0.0 copy-start
  29.5 1.7 copy-done
  31.2 0.1 slice.28
  31.3 12.1 %gather_fusion = bf16[4096,128]{1,0:T(8,128)(2,1)S(1)} fusion(bf16[128,6144]{0,1:T(8,128)(2,1)S(1)} %slice.28, s32[4096]{0:T(1024)S(1)} %bitcast_clamp_fusion), kind=kCustom, calls=%fused_computation | custom fusion | bytes 2113536 | tf_op jit(solution)/shard_map/jit(_take)/gather | solution.py:78
  43.5 0.5 copy.55
  44.0 1.1 select_bitcast_fusion
  45.1 4.9 %all-to-all-start.1 = ((bf16[128,4,1024]{2,0,1:T(8,128)(2,1)}), bf16[128,4,1024]{2,0,1:T(8,128)(2,1)S(1)}, u32[]{:S(2)}, u32[]{:S(2)}) async-start(bf16[128,4,1024]{2,0,1:T(8,128)(2,1)} %select_bitcast_fusion), calls=%async_computation.1 | async-start | bytes 2097152 | tf_op jit(solution)/shard_map/all_to_all | solution.py:79
  50.0 4.7 %copy.65 = bf16[16,4,8,4096]{3,2,0,1:T(8,128)(2,1)} copy(bf16[16,4,8,4096]{3,2,1,0:T(8,128)(2,1)} %bitcast.79) | data formatting | bytes 8388608 | tf_op jit(solution)/shard_map/reshape | solution.py:83
  54.7 22.0 %all-to-all-done.1 = bf16[128,4,1024]{2,0,1:T(8,128)(2,1)S(1)} async-done(((bf16[128,4,1024]{2,0,1:T(8,128)(2,1)}), bf16[128,4,1024]{2,0,1:T(8,128)(2,1)S(1)}, u32[]{:S(2)}, u32[]{:S(2)}) %all-to-all-start.1) | async-done | bytes 1048608 | tf_op jit(solution)/shard_map/all_to_all | solution.py:79
  76.7 0.0 slice-start
  76.7 0.0 copy-start.2
  76.7 5.2 %all-to-all-start = ((bf16[128,4,4096]{2,0,1:T(8,128)(2,1)}), bf16[128,4,4096]{2,0,1:T(8,128)(2,1)}, u32[]{:S(2)}, u32[]{:S(2)}) async-start(bf16[128,4,4096]{2,0,1:T(8,128)(2,1)} %bitcast.76), calls=%async_computation | async-start | bytes 8388608 | tf_op jit(solution)/shard_map/all_to_all | solution.py:86
  81.9 0.0 slice-done
  81.9 3.2 gather_fusion.1
  85.1 0.1 copy.56
  85.3 0.0 copy-done.2
  85.3 0.2 convert_reduce_fusion
  85.5 0.3 fusion.4
  85.8 1.5 multiply_reduce_fusion
  88.0 0.4 fusion.5
  88.4 0.4 convolution_convert_fusion.3
  88.8 0.9 convolution_bitcast_fusion.1
  89.7 0.4 convolution_convert_fusion.2
  90.2 0.4 fusion.6
  90.6 0.4 convolution_convert_fusion.1
  91.1 0.4 convolution_convert_fusion
  91.5 0.4 fusion.7
  92.0 0.4 convolution_divide_fusion
  92.4 1.0 convolution_bitcast_fusion
  93.4 1.0 fusion.19
  94.4 81.2 %all-to-all-done = bf16[128,4,4096]{2,0,1:T(8,128)(2,1)} async-done(((bf16[128,4,4096]{2,0,1:T(8,128)(2,1)}), bf16[128,4,4096]{2,0,1:T(8,128)(2,1)}, u32[]{:S(2)}, u32[]{:S(2)}) %all-to-all-start) | async-done | bytes 4194336 | tf_op jit(solution)/shard_map/all_to_all | solution.py:86
  175.6 3.2 convert_reduce_fusion.1
  178.8 3.1 fusion
  181.8 4.6 %fusion.1 = bf16[512,1,4096]{2,0,1:T(8,128)(2,1)} fusion(bf16[512,4096]{1,0:T(8,128)(2,1)S(1)} %fusion, f32[4096]{0:T(1024)S(1)} %broadcast_multiply_fusion, f32[512,512]{1,0:T(8,128)S(1)} %convolution_divide_fusion, f32[512]{0:T(512)S(1)} %bitcast.82), kind=kOutput, calls=%fused_computation.5 | convolution fusion | flops 2152464384 | bytes 9455616 | tf_op jit(solution)/shard_map/dot_general | solution.py:25
  186.4 0.5 broadcast.126
  186.9 6.6 %reduce.6 = bf16[512,4096]{1,0:T(8,128)(2,1)} reduce(bf16[512,1,4096]{2,0,1:T(8,128)(2,1)} %fusion.1, bf16[]{:T(256)} %broadcast.126), dimensions={1}, to_apply=%copy.57.reduce_sub_computation | reduce | bytes 8388610 | tf_op jit(solution)/shard_map/broadcast_in_dim | solution.py:88
  193.5 6.2 %reshape.136 = bf16[4,2,262144]{2,1,0:T(2,128)(2,1)} reshape(bf16[512,4096]{1,0:T(8,128)(2,1)} %reduce.6) | data formatting | bytes 8388608
  199.7 98.7 %all_to_all.33 = bf16[4,2,262144]{2,1,0:T(2,128)(2,1)} all-to-all(bf16[4,2,262144]{2,1,0:T(2,128)(2,1)} %reshape.136), channel_id=1, replica_groups=mesh['tile'=8,'member'=4] {'member'}, dimensions={0} | all-to-all | bytes 8388608 | tf_op jit(solution)/shard_map/all_to_all | solution.py:88
  298.5 7.4 %reshape.137 = bf16[512,1,4096]{2,1,0:T(2,128)(2,1)} reshape(bf16[4,2,262144]{2,1,0:T(2,128)(2,1)} %all_to_all.33) | data formatting | bytes 8388608
  305.9 10.1 %copy.60 = bf16[512,1,4096]{2,0,1:T(8,128)(2,1)} copy(bf16[512,1,4096]{2,1,0:T(2,128)(2,1)} %reshape.137) | data formatting | bytes 8388608
  316.1 6.3 %copy.58 = bf16[128,4,1,4096]{0,3,1,2:T(8,128)(2,1)} copy(bf16[128,4,1,4096]{3,0,1,2:T(8,128)(2,1)} %bitcast.75) | data formatting | bytes 8388608 | tf_op jit(solution)/shard_map/all_to_all | solution.py:88
  322.4 6.4 %copy.59 = bf16[128,16384]{1,0:T(8,128)(2,1)} copy(bf16[128,16384]{0,1:T(8,128)(2,1)} %bitcast.77) | data formatting | bytes 8388608 | tf_op jit(solution)/shard_map/reshape | solution.py:89
  (10 shorter events, 0.1 us)
Async XLA Ops:
  0.0 8.1 %copy-start.1 = (s32[4,1024]{1,0:T(4,128)S(1)}, s32[4,1024]{1,0:T(4,128)}, u32[]{:S(2)}) copy-start(s32[4,1024]{1,0:T(4,128)} %param.9) | copy-start | bytes 49156
  4.6 13.3 %collective-permute-start = (bf16[130,1024]{0,1:T(8,128)(2,1)S(1)}, bf16[130,1024]{0,1:T(8,128)(2,1)S(1)}, u32[]{:S(2)}, u32[]{:S(2)}) collective-permute-start(bf16[130,1024]{0,1:T(8,128)(2,1)S(1)} %get-tuple-element.7), channel_id=1, source_target_pairs={{0,4},{4,8},{8,12},{12,16},{16,20},{20,24},{24,28},{28,0},{1,5},{5... | collective-permute-start | bytes 798728 | tf_op jit(solution)/shard_map/ppermute | solution.py:16
  5.1 14.2 %collective-permute-start.1 = (bf16[130,1024]{0,1:T(8,128)(2,1)S(1)}, bf16[130,1024]{0,1:T(8,128)(2,1)S(1)}, u32[]{:S(2)}, u32[]{:S(2)}) collective-permute-start(bf16[130,1024]{0,1:T(8,128)(2,1)S(1)} %get-tuple-element.8), channel_id=1, source_target_pairs={{4,0},{8,4},{12,8},{16,12},{20,16},{24,20},{28,24},{0,28},{5,1},{9... | collective-permute-start | bytes 798728 | tf_op jit(solution)/shard_map/ppermute | solution.py:19
  29.5 1.7 copy-start
  45.1 31.6 %all-to-all-start.1 = ((bf16[128,4,1024]{2,0,1:T(8,128)(2,1)}), bf16[128,4,1024]{2,0,1:T(8,128)(2,1)S(1)}, u32[]{:S(2)}, u32[]{:S(2)}) async-start(bf16[128,4,1024]{2,0,1:T(8,128)(2,1)} %select_bitcast_fusion), calls=%async_computation.1 | async-start | bytes 2097152 | tf_op jit(solution)/shard_map/all_to_all | solution.py:79
  76.7 5.2 %slice-start = ((bf16[130,6144]{0,1:T(8,128)(2,1)}), bf16[2,6144]{0,1:T(8,128)(2,1)S(1)}, s32[]{:S(2)}) async-start(bf16[130,6144]{0,1:T(8,128)(2,1)} %copy-done), calls=%async_computation.3 | async-start | bytes 3145728 | tf_op jit(solution)/shard_map/slice | solution.py:77
  76.7 8.6 %copy-start.2 = (f32[1,1024]{1,0:T(1,128)S(1)}, f32[1,1024]{1,0:T(1,128)}, u32[]{:S(2)}) copy-start(f32[1,1024]{1,0:T(1,128)} %param.10) | copy-start | bytes 12292
  76.7 98.9 %all-to-all-start = ((bf16[128,4,4096]{2,0,1:T(8,128)(2,1)}), bf16[128,4,4096]{2,0,1:T(8,128)(2,1)}, u32[]{:S(2)}, u32[]{:S(2)}) async-start(bf16[128,4,4096]{2,0,1:T(8,128)(2,1)} %bitcast.76), calls=%async_computation | async-start | bytes 8388608 | tf_op jit(solution)/shard_map/all_to_all | solution.py:86
where the time goes:
time: 330 us; the launch traced here: 329 us
  waiting for transfers between devices  114 us (35%)
  blocking collectives  98.7 us (30%)
  local copies, waits for them, and re-layouts  63.7 us (19%)
  other arithmetic  25 us (8%)
  starting transfers between devices  13.6 us (4%)
  matrix products  12.4 us (4%)
    all_to_all x1, blocking collectives, on_device(): lax.all_to_all(updated[:, None, :], 'member', split_axis=0, concat_axis=1...  98.7 us
    all_to_all x1, waiting for transfers between devices, on_device(): lax.all_to_all(state_split, 'member', split_axis=1, concat_axis=0, tiled=...  81.2 us
    unnamed x10, local copies, waits for them, and re-layouts  27.1 us
    all_to_all x1, waiting for transfers between devices, on_device(): lax.all_to_all(picked, 'member', split_axis=1, concat_axis=0, tiled=True)  22 us
    gather x2, local copies, waits for them, and re-layouts, on_device(): picked = jnp.take(obs_pool[:ens_dev], obs_index, axis=1)  12.7 us
    concatenate x1, other arithmetic, with_halo(): block = jnp.concatenate([low, block, high], axis=dim)  10.2 us
    ppermute x1, waiting for transfers between devices, with_halo(): lax.ppermute(lax.slice_in_dim(block, block.shape[dim] - width, None, axis...  9.77 us
    dot_general x10, matrix products, product_f32(): lax.dot_general(left.astype(jnp.float32), right.astype(jnp.float32), (dim...  9.54 us
  transfers between devices with their start and end apart: 4, of which 4 were waited for; matrix products, arithmetic and copies ran while one was open for 5% of the time, Pallas kernels for 0%

commit v1 on v0

--- a/solution.py
+++ b/solution.py
@@ -76,7 +76,18 @@
     own_index = lax.dynamic_index_in_dim(obs_index, member_pos, 0, keepdims=False)
     obs_pair = jnp.take(obs_pool[ens_dev:], own_index, axis=1)
     picked = jnp.take(obs_pool[:ens_dev], obs_index, axis=1)
-    received = lax.all_to_all(picked, "member", split_axis=1, concat_axis=0, tiled=True)
+    ways, here = (lax.axis_size("member"), lax.axis_index("member"))
+    width_2 = picked.shape[1] // ways
+    dims_2 = list(picked.shape)
+    dims_2[1] = width_2
+    height = dims_2[0]
+    dims_2[0] = height * ways
+    received = jnp.zeros(dims_2, picked.dtype)
+    for mask in range(ways):
+        part = lax.dynamic_slice_in_dim(picked, (here ^ mask) * width_2, width_2, axis=1)
+        if mask:
+            part = lax.ppermute(part, "member", [(d, d ^ mask) for d in range(ways)])
+        received = lax.dynamic_update_slice_in_dim(received, part, (here ^ mask) * height, axis=0)
     obs_block = received[:, 0, :]
     transform = analysis(obs_block, obs_pair, loc_weight[0])
     group_count = obs_index.shape[0]

time: 330 us -> 297 us (0.900)
  waiting for transfers between devices: 114 us -> 84 us
    all_to_all x1, waiting for transfers between devices: 81.2 us -> 0.01 us  [on_device(): lax.all_to_all(state_split, 'member', split_axis=1, concat_axis=0, tiled=...]
    ppermute x0 -> x3, waiting for transfers between devices: none -> 80.5 us  [on_device(): part = lax.ppermute(part, 'member', [(d, d ^ mask) for d in range(ways)])]
    all_to_all x1 -> x0, waiting for transfers between devices: 22 us -> none  [on_device(): lax.all_to_all(picked, 'member', split_axis=1, concat_axis=0, tiled=True)]
    ppermute x1, waiting for transfers between devices: 9.77 us -> 2.01 us  [with_halo(): lax.ppermute(lax.slice_in_dim(block, block.shape[dim] - width, None, axis...]
    all_to_all x1 -> x0, starting transfers between devices: 4.92 us -> none  [on_device(): lax.all_to_all(picked, 'member', split_axis=1, concat_axis=0, tiled=True)]
    ppermute x0 -> x3, starting transfers between devices: none -> 4.45 us  [on_device(): part = lax.ppermute(part, 'member', [(d, d ^ mask) for d in range(ways)])]
    gather x2 -> x1, local copies, waits for them, and re-layouts: 12.7 us -> 12.1 us  [on_device(): picked = jnp.take(obs_pool[:ens_dev], obs_index, axis=1)]
  transfers between devices with their start and end apart: 4 -> 6, of which waited for: 4 -> 4; matrix products, arithmetic and copies ran while one was open for 5% -> 13% of each run, Pallas kernels for 0% -> 0%
where the time goes in v1:
time: 297 us; the launch traced here: 296 us
  blocking collectives  98.4 us (33%)
  waiting for transfers between devices  84 us (28%)
  local copies, waits for them, and re-layouts  62.3 us (21%)
  other arithmetic  23.6 us (8%)
  starting transfers between devices  13.6 us (5%)
  matrix products  12.9 us (4%)
    all_to_all x1, blocking collectives, on_device(): lax.all_to_all(updated[:, None, :], 'member', split_axis=0, concat_axis=1...  98.4 us
    ppermute x3, waiting for transfers between devices, on_device(): part = lax.ppermute(part, 'member', [(d, d ^ mask) for d in range(ways)])  80.5 us
    unnamed x10, local copies, waits for them, and re-layouts  25.4 us
    gather x1, local copies, waits for them, and re-layouts, on_device(): picked = jnp.take(obs_pool[:ens_dev], obs_index, axis=1)  12.1 us
    dot_general x10, matrix products, product_f32(): lax.dot_general(left.astype(jnp.float32), right.astype(jnp.float32), (dim...  10.2 us
    concatenate x1, other arithmetic, with_halo(): block = jnp.concatenate([low, block, high], axis=dim)  7.28 us
    broadcast_in_dim x1, other arithmetic, on_device(): updated[:, None, :]  6.89 us
    reshape x1, local copies, waits for them, and re-layouts, on_device(): return result.reshape(ens_dev, state.shape[1])  6.36 us
  transfers between devices with their start and end apart: 6, of which 4 were waited for; matrix products, arithmetic and copies ran while one was open for 13% of the time, Pallas kernels for 0%

profile of v1, /device:TPU:0, one launch (start us, length us, event | category | flops | bytes accessed | tf_op | source)
XLA Modules:
  0.0 295.7 jit_solution(2780281211339479976)
XLA Ops:
  0.0 1.6 copy.35
  1.6 0.0 copy-start
  1.6 1.4 broadcast_in_dim.45
  3.1 1.3 broadcast_in_dim.46
  4.4 1.3 pad_maximum_fusion.3
  5.7 0.5 collective-permute-start
  6.2 2.9 collective-permute-start.1
  9.1 0.0 copy-done
  9.1 2.3 copy.48
  11.4 0.0 copy-start.1
  11.4 5.8 %all-to-all-start = ((bf16[128,4,4096]{2,0,1:T(8,128)(2,1)}), bf16[128,4,4096]{2,0,1:T(8,128)(2,1)}, u32[]{:S(2)}, u32[]{:S(2)}) async-start(bf16[128,4,4096]{2,0,1:T(8,128)(2,1)} %bitcast.72), calls=%async_computation | async-start | bytes 8388608 | tf_op jit(solution)/shard_map/all_to_all | solution.py:97
  17.1 0.0 copy-done.1
  17.2 2.0 collective-permute-done
  19.3 1.5 collective-permute-done.1
  20.7 7.3 %pad_maximum_fusion = bf16[130,6144]{0,1:T(8,128)(2,1)S(1)} fusion(bf16[130,1024]{0,1:T(8,128)(2,1)} %collective-permute-done.1, bf16[1,4096]{0,1:T(8,128)(2,1)S(1)} %broadcast_in_dim.46, bf16[1,4096]{0,1:T(8,128)(2,1)S(1)} %broadcast_in_dim.45, bf16[128,4096]{0,1:T(8,128)(2,1)S(1)} %copy.35, bf16[130,1024]{0,1:T(8,128)(2,1)} %collective-permute-done), kind=kLoop, calls=%fused_computation.7 | loop fusion | flops 7987200 | bytes 3194880 | tf_op jit(solution)/shard_map/concatenate | solution.py:20
  28.0 0.1 slice.29
  28.1 0.1 slice.28
  28.2 3.2 %gather_fusion.1 = bf16[1024,2]{1,0:T(8,128)(2,1)S(1)} fusion(bf16[2,6144]{0,1:T(8,128)(2,1)S(1)} %slice.29, s32[1024]{0:T(1024)S(1)} %broadcast_clamp_fusion), kind=kCustom, calls=%fused_computation.1 | custom fusion | bytes 12288 | tf_op jit(solution)/shard_map/jit(_take)/gather | solution.py:77
  31.5 0.2 select_bitcast_fusion
  31.7 0.1 slice.30
  31.8 0.1 copy.38
  31.9 12.1 %gather_fusion = bf16[4096,128]{1,0:T(8,128)(2,1)S(1)} fusion(bf16[128,6144]{0,1:T(8,128)(2,1)S(1)} %slice.28, s32[4096]{0:T(1024)S(1)} %bitcast_clamp_fusion), kind=kCustom, calls=%fused_computation | custom fusion | bytes 2113536 | tf_op jit(solution)/shard_map/jit(_take)/gather | solution.py:78
  44.1 1.2 broadcast_select_fusion
  45.3 0.1 dynamic-slice_bitcast_fusion
  45.4 3.7 %collective-permute-start.4 = (bf16[128,1,1024]{0,2,1:T(8,128)(2,1)S(1)}, bf16[128,1,1024]{0,2,1:T(8,128)(2,1)S(1)}, u32[]{:S(2)}, u32[]{:S(2)}) collective-permute-start(bf16[128,1,1024]{0,2,1:T(8,128)(2,1)S(1)} %get-tuple-element.9), channel_id=1, source_target_pairs={{0,3},{1,2},{2,1},{3,0},{4,7},{5,6},{6,5},{7,4},{8,11},{9,10},{10,... | collective-permute-start | bytes 786440 | tf_op jit(solution)/shard_map/ppermute | solution.py:89
  49.1 0.0 collective-permute-start.3
  49.1 0.7 collective-permute-start.2
  49.8 0.1 convert_reduce_fusion.2
  50.0 0.0 copy-done.2
  50.0 0.2 copy.39
  50.2 0.2 sqrt_reduce_fusion
  50.5 0.1 squeeze.21
  50.6 0.1 bitcast_dynamic-update-slice_fusion
  50.6 50.3 %collective-permute-done.2 = bf16[128,1,1024]{0,2,1:T(8,128)(2,1)} collective-permute-done((bf16[128,1,1024]{0,2,1:T(8,128)(2,1)S(1)}, bf16[128,1,1024]{0,2,1:T(8,128)(2,1)}, u32[]{:S(2)}, u32[]{:S(2)}) %collective-permute-start.2) | collective-permute-done | bytes 262176 | tf_op jit(solution)/shard_map/ppermute | solution.py:89
  101.0 1.0 bitcast_dynamic-update-slice_fusion.3
  102.0 30.2 %collective-permute-done.3 = bf16[128,1,1024]{0,2,1:T(8,128)(2,1)} collective-permute-done((bf16[128,1,1024]{0,2,1:T(8,128)(2,1)S(1)}, bf16[128,1,1024]{0,2,1:T(8,128)(2,1)}, u32[]{:S(2)}, u32[]{:S(2)}) %collective-permute-start.3) | collective-permute-done | bytes 262176 | tf_op jit(solution)/shard_map/ppermute | solution.py:89
  132.2 1.0 bitcast_dynamic-update-slice_fusion.2
  133.2 0.0 collective-permute-done.4
  133.2 0.1 bitcast_dynamic-update-slice_fusion.1
  133.3 0.2 convert_reduce_fusion
  133.5 2.1 multiply_reduce_fusion
  136.3 0.4 fusion.4
  136.8 0.4 convolution_convert_fusion.3
  137.2 0.7 convolution_bitcast_fusion.1
  137.9 0.4 convolution_convert_fusion.2
  138.4 0.4 fusion.5
  138.8 0.4 convolution_convert_fusion.1
  139.3 0.4 convolution_convert_fusion
  139.7 0.4 fusion.6
  140.2 0.4 convolution_divide_fusion
  140.6 1.0 convolution_bitcast_fusion
  141.6 1.0 fusion.13
  142.6 0.0 all-to-all-done
  142.6 3.2 %convert_reduce_fusion.1 = f32[4096]{0:T(1024)S(1)} fusion(bf16[128,4,4096]{2,0,1:T(8,128)(2,1)} %all-to-all-done), kind=kLoop, calls=%fused_computation.12 | loop fusion | flops 4190208 | bytes 4210688 | tf_op jit(solution)/shard_map/reduce_sum | solution.py:65
  145.8 3.1 %fusion = bf16[512,4096]{1,0:T(8,128)(2,1)S(1)} fusion(f32[4096]{0:T(1024)S(1)} %broadcast_multiply_fusion, bf16[128,4,4096]{2,0,1:T(8,128)(2,1)} %all-to-all-done), kind=kLoop, calls=%fused_computation.3 | loop fusion | flops 6291456 | bytes 8404992 | tf_op jit(solution)/shard_map/convert_element_type | solution.py:66
  148.9 4.6 %fusion.1 = bf16[512,1,4096]{2,0,1:T(8,128)(2,1)} fusion(bf16[512,4096]{1,0:T(8,128)(2,1)S(1)} %fusion, f32[4096]{0:T(1024)S(1)} %broadcast_multiply_fusion, f32[512,512]{1,0:T(8,128)S(1)} %convolution_divide_fusion, f32[512]{0:T(512)S(1)} %bitcast.76), kind=kOutput, calls=%fused_computation.5 | convolution fusion | flops 2152464384 | bytes 9455616 | tf_op jit(solution)/shard_map/dot_general | solution.py:25
  153.4 0.5 broadcast.83
  153.9 6.9 %reduce.7 = bf16[512,4096]{1,0:T(8,128)(2,1)} reduce(bf16[512,1,4096]{2,0,1:T(8,128)(2,1)} %fusion.1, bf16[]{:T(256)} %broadcast.83), dimensions={1}, to_apply=%copy.40.reduce_sub_computation | reduce | bytes 8388610 | tf_op jit(solution)/shard_map/broadcast_in_dim | solution.py:99
  160.8 6.2 %reshape.103 = bf16[4,2,262144]{2,1,0:T(2,128)(2,1)} reshape(bf16[512,4096]{1,0:T(8,128)(2,1)} %reduce.7) | data formatting | bytes 8388608
  167.0 98.4 %all_to_all.24 = bf16[4,2,262144]{2,1,0:T(2,128)(2,1)} all-to-all(bf16[4,2,262144]{2,1,0:T(2,128)(2,1)} %reshape.103), channel_id=1, replica_groups=mesh['tile'=8,'member'=4] {'member'}, dimensions={0} | all-to-all | bytes 8388608 | tf_op jit(solution)/shard_map/all_to_all | solution.py:99
  265.4 7.4 %reshape.104 = bf16[512,1,4096]{2,1,0:T(2,128)(2,1)} reshape(bf16[4,2,262144]{2,1,0:T(2,128)(2,1)} %all_to_all.24) | data formatting | bytes 8388608
  272.9 10.1 %copy.43 = bf16[512,1,4096]{2,0,1:T(8,128)(2,1)} copy(bf16[512,1,4096]{2,1,0:T(2,128)(2,1)} %reshape.104) | data formatting | bytes 8388608
  283.0 6.3 %copy.41 = bf16[128,4,1,4096]{0,3,1,2:T(8,128)(2,1)} copy(bf16[128,4,1,4096]{3,0,1,2:T(8,128)(2,1)} %bitcast.71) | data formatting | bytes 8388608 | tf_op jit(solution)/shard_map/all_to_all | solution.py:99
  289.3 6.4 %copy.42 = bf16[128,16384]{1,0:T(8,128)(2,1)} copy(bf16[128,16384]{0,1:T(8,128)(2,1)} %bitcast.73) | data formatting | bytes 8388608 | tf_op jit(solution)/shard_map/reshape | solution.py:100
  (10 shorter events, 0.1 us)
Async XLA Ops:
  1.6 7.4 %copy-start = (bf16[128,16384]{1,0:T(8,128)(2,1)S(1)}, bf16[128,16384]{1,0:T(8,128)(2,1)}, u32[]{:S(2)}) copy-start(bf16[128,16384]{1,0:T(8,128)(2,1)} %param.11) | copy-start | bytes 12582916
  5.7 13.6 %collective-permute-start = (bf16[130,1024]{0,1:T(8,128)(2,1)}, bf16[130,1024]{0,1:T(8,128)(2,1)}, u32[]{:S(2)}, u32[]{:S(2)}) collective-permute-start(bf16[130,1024]{0,1:T(8,128)(2,1)} %get-tuple-element.7), channel_id=1, source_target_pairs={{0,4},{4,8},{8,12},{12,16},{16,20},{20,24},{24,28},{28,0},{1,5},{5... | collective-permute-start | bytes 798728 | tf_op jit(solution)/shard_map/ppermute | solution.py:16
  6.2 14.5 %collective-permute-start.1 = (bf16[130,1024]{0,1:T(8,128)(2,1)}, bf16[130,1024]{0,1:T(8,128)(2,1)}, u32[]{:S(2)}, u32[]{:S(2)}) collective-permute-start(bf16[130,1024]{0,1:T(8,128)(2,1)} %get-tuple-element.8), channel_id=1, source_target_pairs={{4,0},{8,4},{12,8},{16,12},{20,16},{24,20},{28,24},{0,28},{5,1},{9... | collective-permute-start | bytes 798728 | tf_op jit(solution)/shard_map/ppermute | solution.py:19
  11.4 5.8 %copy-start.1 = (s32[4,1024]{1,0:T(4,128)S(1)}, s32[4,1024]{1,0:T(4,128)}, u32[]{:S(2)}) copy-start(s32[4,1024]{1,0:T(4,128)} %param.9) | copy-start | bytes 49156
  11.4 131.2 %all-to-all-start = ((bf16[128,4,4096]{2,0,1:T(8,128)(2,1)}), bf16[128,4,4096]{2,0,1:T(8,128)(2,1)}, u32[]{:S(2)}, u32[]{:S(2)}) async-start(bf16[128,4,4096]{2,0,1:T(8,128)(2,1)} %bitcast.72), calls=%async_computation | async-start | bytes 8388608 | tf_op jit(solution)/shard_map/all_to_all | solution.py:97
  31.9 18.1 %copy-start.2 = (f32[1,1024]{1,0:T(1,128)S(1)}, f32[1,1024]{1,0:T(1,128)}, u32[]{:S(2)}) copy-start(f32[1,1024]{1,0:T(1,128)} %param.10) | copy-start | bytes 12292
  45.4 87.8 %collective-permute-start.4 = (bf16[128,1,1024]{0,2,1:T(8,128)(2,1)S(1)}, bf16[128,1,1024]{0,2,1:T(8,128)(2,1)S(1)}, u32[]{:S(2)}, u32[]{:S(2)}) collective-permute-start(bf16[128,1,1024]{0,2,1:T(8,128)(2,1)S(1)} %get-tuple-element.9), channel_id=1, source_target_pairs={{0,3},{1,2},{2,1},{3,0},{4,7},{5,6},{6,5},{7,4},{8,11},{9,10},{10,... | collective-permute-start | bytes 786440 | tf_op jit(solution)/shard_map/ppermute | solution.py:89
  49.1 83.1 %collective-permute-start.3 = (bf16[128,1,1024]{0,2,1:T(8,128)(2,1)S(1)}, bf16[128,1,1024]{0,2,1:T(8,128)(2,1)}, u32[]{:S(2)}, u32[]{:S(2)}) collective-permute-start(bf16[128,1,1024]{0,2,1:T(8,128)(2,1)S(1)} %get-tuple-element.10), channel_id=1, source_target_pairs={{0,2},{1,3},{2,0},{3,1},{4,6},{5,7},{6,4},{7,5},{8,10},{9,11},{10,... | collective-permute-start | bytes 786440 | tf_op jit(solution)/shard_map/ppermute | solution.py:89
  49.1 51.8 %collective-permute-start.2 = (bf16[128,1,1024]{0,2,1:T(8,128)(2,1)S(1)}, bf16[128,1,1024]{0,2,1:T(8,128)(2,1)}, u32[]{:S(2)}, u32[]{:S(2)}) collective-permute-start(bf16[128,1,1024]{0,2,1:T(8,128)(2,1)S(1)} %get-tuple-element.11), channel_id=1, source_target_pairs={{0,1},{1,0},{2,3},{3,2},{4,5},{5,4},{6,7},{7,6},{8,9},{9,8},{10,11... | collective-permute-start | bytes 786440 | tf_op jit(solution)/shard_map/ppermute | solution.py:89
